TPU v7x, 128 devices: a whole 4x4x4 slice. The times are simulated.
128 devices in a mesh: section: 8 (over y, core), edge: 16 (over z, x).
Axes of the slice: x: 4, y: 4, z: 4, core: 2. Of those that a mesh axis runs over, the one named last changes fastest.
Arguments:
- layer_nodes: bfloat16 [8, 2, 256, 512], P('section'), may hold values from -6 to 6
- layer_edges: bfloat16 [8, 2, 4096, 512], P('section', None, 'edge'), may hold values from -6 to 6
- top_nodes: bfloat16 [2, 256, 512], replicated, may hold values from -1.5 to 1.5
- top_edges: bfloat16 [2, 4096, 512], P(None, 'edge'), may hold values from -1.5 to 1.5
- tile_blocks: int32 [2, 32, 2], P(None, 'edge'), may hold values from 0 to 1
- senders: int32 [2, 4096], P(None, 'edge'), may hold values from 0 to 127
- receivers: int32 [2, 4096], P(None, 'edge'), may hold values from 0 to 127
- w_send: bfloat16 [8, 512, 512], P('section'), may hold values from -0.0625 to 0.0625
- w_recv: bfloat16 [8, 512, 512], P('section'), may hold values from -0.0625 to 0.0625
- w_edge: bfloat16 [8, 512, 512], P('section'), may hold values from -0.25 to 0.25
- w_msg: bfloat16 [8, 512, 512], P('section'), may hold values from -0.125 to 0.125
- w_node: bfloat16 [8, 512, 512], P('section'), may hold values from -0.25 to 0.25
- w_agg: bfloat16 [8, 512, 512], P('section'), may hold values from -0.25 to 0.25
- w_out: bfloat16 [8, 512, 512], P('section'), may hold values from -0.125 to 0.125
Outputs:
- node_grads: bfloat16 [8, 2, 256, 512], P('section', None, 'edge')
- edge_grads: bfloat16 [8, 2, 4096, 512], P('section', None, 'edge')
- g_send: float32 [8, 512, 512], P('section', 'edge')
- g_recv: float32 [8, 512, 512], P('section', 'edge')
- g_edge: float32 [8, 512, 512], P('section', 'edge')
- g_msg: float32 [8, 512, 512], P('section', 'edge')
- g_node: float32 [8, 512, 512], P('section', 'edge')
- g_agg: float32 [8, 512, 512], P('section', 'edge')
- g_out: float32 [8, 512, 512], P('section', 'edge')
All inputs are finite; a program needn't handle non-finite values.
Results may differ from a plain program's by a relative error of at most 0.029.
Values may be sent and summed in bfloat16 or wider, within the bound.
A program may use at most 64 MiB of HBM per device.

v0:
```python
import jax
import jax.numpy as jnp
from jax import lax
from jax.sharding import PartitionSpec as P

BLOCK = 128


def shifted(shard, axis, by):
    peers = lax.axis_size(axis)
    pairs = [(i, i + by) for i in range(peers) if 0 <= i + by < peers]
    return lax.ppermute(shard, axis, pairs)


def silu_slope(values):
    sigma = jax.nn.sigmoid(values)
    return sigma * (1.0 + values * (1.0 - sigma))


def matmul(left, right):
    return jnp.dot(left, right, preferred_element_type=jnp.float32)


def times_transposed(left, right):
    return lax.dot_general(
        left, right, (((1,), (1,)), ((), ())), preferred_element_type=jnp.float32
    )


def transposed_times(left, right):
    return lax.dot_general(
        left, right, (((0,), (0,)), ((), ())), preferred_element_type=jnp.float32
    )


def to_edges(values, block_hot, edge_hot):
    width = values.shape[1]
    grouped = values.reshape(block_hot.shape[1], -1, width)
    picked = jnp.einsum(
        "tb,bcd->tcd", block_hot, grouped, preferred_element_type=jnp.float32
    ).astype(jnp.bfloat16)
    spread = jnp.einsum("tec,tcd->ted", edge_hot, picked, preferred_element_type=jnp.float32)
    return spread.reshape(-1, width).astype(jnp.bfloat16)


def to_nodes(values, block_hot, edge_hot):
    width = values.shape[1]
    per_tile = jnp.einsum(
        "tec,ted->tcd",
        edge_hot,
        values.reshape(block_hot.shape[0], -1, width),
        preferred_element_type=jnp.float32,
    )
    summed = jnp.einsum(
        "tb,tcd->bcd", block_hot.astype(jnp.float32), per_tile, precision=lax.Precision.HIGHEST
    )
    return summed.reshape(-1, width)


def body(
    layer_nodes,
    layer_edges,
    top_nodes,
    top_edges,
    tile_blocks,
    senders,
    receivers,
    w_send,
    w_recv,
    w_edge,
    w_msg,
    w_node,
    w_agg,
    w_out,
):
    sections = lax.axis_size("section")
    section = lax.axis_index("section")
    groups = lax.axis_size("edge")
    member = lax.axis_index("edge")
    nodes_all = layer_nodes[0]
    edges_all = layer_edges[0]
    batches = nodes_all.shape[0]
    node_count = nodes_all.shape[1]
    width = nodes_all.shape[2]
    tile_count = tile_blocks.shape[1]
    tile_len = edges_all.shape[1] // tile_count
    block_count = node_count // BLOCK
    row_count = node_count // groups
    weight_send, weight_recv, weight_edge, weight_msg = (w_send[0], w_recv[0], w_edge[0], w_msg[0])
    weight_node, weight_agg, weight_out = (w_node[0], w_agg[0], w_out[0])
    lanes = jnp.arange(BLOCK, dtype=jnp.int32)
    slots = jnp.arange(block_count, dtype=jnp.int32)
    send_hot = (senders.reshape(batches, tile_count, tile_len)[..., None] == lanes).astype(
        jnp.bfloat16
    )
    recv_hot = (receivers.reshape(batches, tile_count, tile_len)[..., None] == lanes).astype(
        jnp.bfloat16
    )
    send_block = (tile_blocks[:, :, 0][..., None] == slots).astype(jnp.bfloat16)
    recv_block = (tile_blocks[:, :, 1][..., None] == slots).astype(jnp.bfloat16)

    def advance(moment, carry):
        node_in_grad, edge_in_grad, totals, node_record, edge_record = carry
        batch_raw = moment - (sections - 1 - section)
        valid = (batch_raw >= 0) & (batch_raw < batches)
        batch = jnp.clip(batch_raw, 0, batches - 1)
        feats = lax.dynamic_index_in_dim(nodes_all, batch, 0, keepdims=False)
        edge_feats = lax.dynamic_index_in_dim(edges_all, batch, 0, keepdims=False)
        send_tiles = lax.dynamic_index_in_dim(send_hot, batch, 0, keepdims=False)
        recv_tiles = lax.dynamic_index_in_dim(recv_hot, batch, 0, keepdims=False)
        send_blocks = lax.dynamic_index_in_dim(send_block, batch, 0, keepdims=False)
        recv_blocks = lax.dynamic_index_in_dim(recv_block, batch, 0, keepdims=False)
        top_node = lax.dynamic_index_in_dim(top_nodes, batch, 0, keepdims=False)
        top_edge = lax.dynamic_index_in_dim(top_edges, batch, 0, keepdims=False)
        is_last = section == sections - 1
        grad_nodes = jnp.where(is_last, top_node, node_in_grad)
        grad_edges = jnp.where(is_last, top_edge, edge_in_grad)
        send_feats = to_edges(feats, send_blocks, send_tiles)
        recv_feats = to_edges(feats, recv_blocks, recv_tiles)
        pre = (
            matmul(send_feats, weight_send)
            + matmul(recv_feats, weight_recv)
            + matmul(edge_feats, weight_edge)
        )
        act = jax.nn.silu(pre).astype(jnp.bfloat16)
        message = matmul(act, weight_msg).astype(jnp.bfloat16)
        partial_agg = to_nodes(message, recv_blocks, recv_tiles)
        aggregate = lax.psum(partial_agg, "edge")
        agg_b = aggregate.astype(jnp.bfloat16)
        node_pre = matmul(feats, weight_node) + matmul(agg_b, weight_agg)
        node_act = jax.nn.silu(node_pre).astype(jnp.bfloat16)
        node_delta = (times_transposed(grad_nodes, weight_out) * silu_slope(node_pre)).astype(
            jnp.bfloat16
        )
        agg_grad = times_transposed(node_delta, weight_agg).astype(jnp.bfloat16)
        node_term = times_transposed(node_delta, weight_node)
        agg_edges = to_edges(agg_grad, recv_blocks, recv_tiles)
        message_grad = (grad_edges.astype(jnp.float32) + agg_edges.astype(jnp.float32)).astype(
            jnp.bfloat16
        )
        edge_delta = (times_transposed(message_grad, weight_msg) * silu_slope(pre)).astype(
            jnp.bfloat16
        )
        edge_out = (
            grad_edges.astype(jnp.float32) + times_transposed(edge_delta, weight_edge)
        ).astype(jnp.bfloat16)
        send_grad = times_transposed(edge_delta, weight_send).astype(jnp.bfloat16)
        recv_grad = times_transposed(edge_delta, weight_recv).astype(jnp.bfloat16)
        partial_back = to_nodes(send_grad, send_blocks, send_tiles) + to_nodes(
            recv_grad, recv_blocks, recv_tiles
        )
        edge_terms = lax.psum(partial_back, "edge")
        node_out = (grad_nodes.astype(jnp.float32) + node_term + edge_terms).astype(jnp.bfloat16)
        fresh = (
            transposed_times(send_feats, edge_delta),
            transposed_times(recv_feats, edge_delta),
            transposed_times(edge_feats, edge_delta),
            transposed_times(act, message_grad),
            transposed_times(feats, node_delta),
            transposed_times(agg_b, node_delta),
            transposed_times(node_act, grad_nodes),
        )
        totals = tuple(
            (jnp.where(valid, before + extra, before) for before, extra in zip(totals, fresh))
        )
        own_out = lax.dynamic_slice_in_dim(node_out, member * row_count, row_count, 0)
        node_record = jnp.where(
            valid, lax.dynamic_update_index_in_dim(node_record, own_out, batch, 0), node_record
        )
        edge_record = jnp.where(
            valid, lax.dynamic_update_index_in_dim(edge_record, edge_out, batch, 0), edge_record
        )
        sent_nodes, sent_edges = shifted((node_out, edge_out), "section", -1)
        return (sent_nodes, sent_edges, totals, node_record, edge_record)

    hidden = weight_send.shape[1]
    square_in = jnp.zeros((width, hidden), jnp.float32)
    square_back = jnp.zeros((hidden, width), jnp.float32)
    start = (
        jnp.zeros((node_count, width), jnp.bfloat16),
        jnp.zeros(edges_all.shape[1:], jnp.bfloat16),
        (square_in, square_in, square_in, square_back, square_in, square_in, square_back),
        jnp.zeros((batches, row_count, width), jnp.bfloat16),
        jnp.zeros(edges_all.shape, jnp.bfloat16),
    )
    finished = lax.fori_loop(0, sections + batches - 1, advance, start)
    totals, node_record, edge_record = (finished[2], finished[3], finished[4])
    sum_send, sum_recv, sum_edge, sum_msg, sum_node, sum_agg, sum_out = totals
    sum_send, sum_recv, sum_edge, sum_msg = (
        lax.psum_scatter(sum_send, "edge", scatter_dimension=0, tiled=True),
        lax.psum_scatter(sum_recv, "edge", scatter_dimension=0, tiled=True),
        lax.psum_scatter(sum_edge, "edge", scatter_dimension=0, tiled=True),
        lax.psum_scatter(sum_msg, "edge", scatter_dimension=0, tiled=True),
    )
    sum_node = lax.dynamic_slice_in_dim(sum_node, member * (width // groups), width // groups, 0)
    sum_agg = lax.dynamic_slice_in_dim(sum_agg, member * (width // groups), width // groups, 0)
    sum_out = lax.dynamic_slice_in_dim(sum_out, member * (hidden // groups), hidden // groups, 0)
    return (
        node_record[None],
        edge_record[None],
        sum_send[None],
        sum_recv[None],
        sum_edge[None],
        sum_msg[None],
        sum_node[None],
        sum_agg[None],
        sum_out[None],
    )


def solution(mesh):
    in_specs = (
        P("section", None, None, None),
        P("section", None, "edge", None),
        P(),
        P(None, "edge", None),
        P(None, "edge", None),
        P(None, "edge"),
        P(None, "edge"),
        P("section", None, None),
        P("section", None, None),
        P("section", None, None),
        P("section", None, None),
        P("section", None, None),
        P("section", None, None),
        P("section", None, None),
    )
    out_specs = (
        P("section", None, "edge", None),
        P("section", None, "edge", None),
        P("section", "edge", None),
        P("section", "edge", None),
        P("section", "edge", None),
        P("section", "edge", None),
        P("section", "edge", None),
        P("section", "edge", None),
        P("section", "edge", None),
    )
    return jax.shard_map(body, mesh=mesh, in_specs=in_specs, out_specs=out_specs, check_vma=False)
```

profile of v0, /device:TPU:0, one launch (start us, length us, event | category | flops | bytes accessed | tf_op | source)
XLA Modules:
  0.0 2031.3 jit_solution(16253940211328947030)
XLA Ops:
  13.3 1701.8 %while.36 = (s32[]{:T(128)}, bf16[256,512]{1,0:T(8,128)(2,1)S(1)}, bf16[256,512]{1,0:T(8,128)(2,1)S(1)}, f32[512,512]{1,0:T(8,128)}, f32[512,512]{1,0:T(8,128)},...) while((s32[]{:T(128)}, bf16[256,512]{1,0:T(8,128)(2,1)S(1)}, ...), condition=%wide.region_3.4_spmd.clone, body=%wide.region_0.3_spmd.clone.sunk | while | flops 2910199808 | bytes 137546704 | solution.py:186
  21.1 81.4 %all-reduce.4 = bf16[256,512]{1,0:T(8,128)(2,1)S(1)} all-reduce(f32[256,512]{1,0:T(8,128)S(1)} %bitcast.271), channel_id=1, replica_groups=mesh['section'=8,'edge'=16] {'edge'}, use_global_device_ids=true, to_apply=%region_1.1 | all-reduce | flops 131072 | bytes 786432 | tf_op jit(solution)/shard_map/while/body/eval_jaxpr/psum | solution.py:128
  113.3 1.5 convolution_add_fusion.13
  116.8 2.2 fusion.248
  120.3 2.6 add_select_fusion.17
  129.5 69.2 %all-reduce.3.cloned.1.call-done = f32[256,512]{1,0:T(8,128)} async-done(((f32[256,512]{1,0:T(8,128)}), f32[256,512]{1,0:T(8,128)}) %all-reduce.3.cloned.1.call-update) | async-done | bytes 524304 | tf_op jit(solution)/shard_map/while/body/eval_jaxpr/psum | solution.py:152
  198.6 1.4 fusion.247
  211.4 77.6 %all-reduce.4 = bf16[256,512]{1,0:T(8,128)(2,1)S(1)} all-reduce(f32[256,512]{1,0:T(8,128)S(1)} %bitcast.271), channel_id=1, replica_groups=mesh['section'=8,'edge'=16] {'edge'}, use_global_device_ids=true, to_apply=%region_1.1 | all-reduce | flops 131072 | bytes 786432 | tf_op jit(solution)/shard_map/while/body/eval_jaxpr/psum | solution.py:128
  299.8 1.5 convolution_add_fusion.13
  303.3 2.2 fusion.248
  306.7 2.9 add_select_fusion.17
  314.9 2.6 add_select_fusion.20
  317.5 70.1 %all-reduce.3.cloned.1.call-done = f32[256,512]{1,0:T(8,128)} async-done(((f32[256,512]{1,0:T(8,128)}), f32[256,512]{1,0:T(8,128)}) %all-reduce.3.cloned.1.call-update) | async-done | bytes 524304 | tf_op jit(solution)/shard_map/while/body/eval_jaxpr/psum | solution.py:152
  387.6 1.4 fusion.247
  400.3 77.6 %all-reduce.4 = bf16[256,512]{1,0:T(8,128)(2,1)S(1)} all-reduce(f32[256,512]{1,0:T(8,128)S(1)} %bitcast.271), channel_id=1, replica_groups=mesh['section'=8,'edge'=16] {'edge'}, use_global_device_ids=true, to_apply=%region_1.1 | all-reduce | flops 131072 | bytes 786432 | tf_op jit(solution)/shard_map/while/body/eval_jaxpr/psum | solution.py:128
  488.7 1.5 convolution_add_fusion.13
  492.2 2.2 fusion.248
  495.7 2.9 add_select_fusion.17
  503.9 2.6 add_select_fusion.20
  506.5 70.1 %all-reduce.3.cloned.1.call-done = f32[256,512]{1,0:T(8,128)} async-done(((f32[256,512]{1,0:T(8,128)}), f32[256,512]{1,0:T(8,128)}) %all-reduce.3.cloned.1.call-update) | async-done | bytes 524304 | tf_op jit(solution)/shard_map/while/body/eval_jaxpr/psum | solution.py:152
  576.5 1.4 fusion.247
  589.3 77.6 %all-reduce.4 = bf16[256,512]{1,0:T(8,128)(2,1)S(1)} all-reduce(f32[256,512]{1,0:T(8,128)S(1)} %bitcast.271), channel_id=1, replica_groups=mesh['section'=8,'edge'=16] {'edge'}, use_global_device_ids=true, to_apply=%region_1.1 | all-reduce | flops 131072 | bytes 786432 | tf_op jit(solution)/shard_map/while/body/eval_jaxpr/psum | solution.py:128
  677.7 1.5 convolution_add_fusion.13
  681.2 2.2 fusion.248
  684.6 2.9 add_select_fusion.17
  692.8 2.6 add_select_fusion.20
  695.4 70.1 %all-reduce.3.cloned.1.call-done = f32[256,512]{1,0:T(8,128)} async-done(((f32[256,512]{1,0:T(8,128)}), f32[256,512]{1,0:T(8,128)}) %all-reduce.3.cloned.1.call-update) | async-done | bytes 524304 | tf_op jit(solution)/shard_map/while/body/eval_jaxpr/psum | solution.py:152
  778.2 77.6 %all-reduce.4 = bf16[256,512]{1,0:T(8,128)(2,1)S(1)} all-reduce(f32[256,512]{1,0:T(8,128)S(1)} %bitcast.271), channel_id=1, replica_groups=mesh['section'=8,'edge'=16] {'edge'}, use_global_device_ids=true, to_apply=%region_1.1 | all-reduce | flops 131072 | bytes 786432 | tf_op jit(solution)/shard_map/while/body/eval_jaxpr/psum | solution.py:128
  866.6 1.5 convolution_add_fusion.13
  870.1 2.2 fusion.248
  873.6 2.9 add_select_fusion.17
  881.8 2.6 add_select_fusion.20
  884.4 70.1 %all-reduce.3.cloned.1.call-done = f32[256,512]{1,0:T(8,128)} async-done(((f32[256,512]{1,0:T(8,128)}), f32[256,512]{1,0:T(8,128)}) %all-reduce.3.cloned.1.call-update) | async-done | bytes 524304 | tf_op jit(solution)/shard_map/while/body/eval_jaxpr/psum | solution.py:152
  967.2 77.6 %all-reduce.4 = bf16[256,512]{1,0:T(8,128)(2,1)S(1)} all-reduce(f32[256,512]{1,0:T(8,128)S(1)} %bitcast.271), channel_id=1, replica_groups=mesh['section'=8,'edge'=16] {'edge'}, use_global_device_ids=true, to_apply=%region_1.1 | all-reduce | flops 131072 | bytes 786432 | tf_op jit(solution)/shard_map/while/body/eval_jaxpr/psum | solution.py:128
  1055.6 1.5 convolution_add_fusion.13
  1059.1 2.2 fusion.248
  1062.5 2.9 add_select_fusion.17
  1070.7 2.6 add_select_fusion.20
  1073.3 70.1 %all-reduce.3.cloned.1.call-done = f32[256,512]{1,0:T(8,128)} async-done(((f32[256,512]{1,0:T(8,128)}), f32[256,512]{1,0:T(8,128)}) %all-reduce.3.cloned.1.call-update) | async-done | bytes 524304 | tf_op jit(solution)/shard_map/while/body/eval_jaxpr/psum | solution.py:152
  1156.1 77.6 %all-reduce.4 = bf16[256,512]{1,0:T(8,128)(2,1)S(1)} all-reduce(f32[256,512]{1,0:T(8,128)S(1)} %bitcast.271), channel_id=1, replica_groups=mesh['section'=8,'edge'=16] {'edge'}, use_global_device_ids=true, to_apply=%region_1.1 | all-reduce | flops 131072 | bytes 786432 | tf_op jit(solution)/shard_map/while/body/eval_jaxpr/psum | solution.py:128
  1244.5 1.5 convolution_add_fusion.13
  1248.0 2.2 fusion.248
  1251.5 2.9 add_select_fusion.17
  1259.7 2.6 add_select_fusion.20
  1262.3 70.1 %all-reduce.3.cloned.1.call-done = f32[256,512]{1,0:T(8,128)} async-done(((f32[256,512]{1,0:T(8,128)}), f32[256,512]{1,0:T(8,128)}) %all-reduce.3.cloned.1.call-update) | async-done | bytes 524304 | tf_op jit(solution)/shard_map/while/body/eval_jaxpr/psum | solution.py:152
  1345.1 77.6 %all-reduce.4 = bf16[256,512]{1,0:T(8,128)(2,1)S(1)} all-reduce(f32[256,512]{1,0:T(8,128)S(1)} %bitcast.271), channel_id=1, replica_groups=mesh['section'=8,'edge'=16] {'edge'}, use_global_device_ids=true, to_apply=%region_1.1 | all-reduce | flops 131072 | bytes 786432 | tf_op jit(solution)/shard_map/while/body/eval_jaxpr/psum | solution.py:128
  1433.5 1.5 convolution_add_fusion.13
  1437.0 2.2 fusion.248
  1440.4 2.9 add_select_fusion.17
  1448.6 2.6 add_select_fusion.20
  1451.2 70.1 %all-reduce.3.cloned.1.call-done = f32[256,512]{1,0:T(8,128)} async-done(((f32[256,512]{1,0:T(8,128)}), f32[256,512]{1,0:T(8,128)}) %all-reduce.3.cloned.1.call-update) | async-done | bytes 524304 | tf_op jit(solution)/shard_map/while/body/eval_jaxpr/psum | solution.py:152
  1534.1 77.6 %all-reduce.4 = bf16[256,512]{1,0:T(8,128)(2,1)S(1)} all-reduce(f32[256,512]{1,0:T(8,128)S(1)} %bitcast.271), channel_id=1, replica_groups=mesh['section'=8,'edge'=16] {'edge'}, use_global_device_ids=true, to_apply=%region_1.1 | all-reduce | flops 131072 | bytes 786432 | tf_op jit(solution)/shard_map/while/body/eval_jaxpr/psum | solution.py:128
  1622.4 1.5 convolution_add_fusion.13
  1625.9 2.2 fusion.248
  1629.4 2.9 add_select_fusion.17
  1637.6 2.6 add_select_fusion.20
  1640.2 70.1 %all-reduce.3.cloned.1.call-done = f32[256,512]{1,0:T(8,128)} async-done(((f32[256,512]{1,0:T(8,128)}), f32[256,512]{1,0:T(8,128)}) %all-reduce.3.cloned.1.call-update) | async-done | bytes 524304 | tf_op jit(solution)/shard_map/while/body/eval_jaxpr/psum | solution.py:152
  1717.6 1.5 dynamic-slice_bitcast_fusion
  1719.1 1.5 dynamic-slice_bitcast_fusion.2
  1720.6 1.5 dynamic-slice_bitcast_fusion.1
  1722.0 73.1 %reduce-scatter.5.cloned.1.call-done = f32[32,512]{1,0:T(8,128)} async-done(((f32[512,512]{1,0:T(8,128)}), f32[32,512]{1,0:T(8,128)}) %reduce-scatter.5.cloned.1.call-update) | async-done | bytes 65552 | tf_op jit(solution)/shard_map/reduce_scatter | solution.py:190
  1795.1 76.3 %reduce-scatter.7.cloned.1.call-done = f32[32,512]{1,0:T(8,128)} async-done(((f32[512,512]{1,0:T(8,128)}), f32[32,512]{1,0:T(8,128)}) %reduce-scatter.7.cloned.1.call-update) | async-done | bytes 65552 | tf_op jit(solution)/shard_map/reduce_scatter | solution.py:191
  1871.4 76.0 %reduce-scatter.9.cloned.1.call-done = f32[32,512]{1,0:T(8,128)} async-done(((f32[512,512]{1,0:T(8,128)}), f32[32,512]{1,0:T(8,128)}) %reduce-scatter.9.cloned.1.call-update) | async-done | bytes 65552 | tf_op jit(solution)/shard_map/reduce_scatter | solution.py:192
  1947.4 76.5 %reduce-scatter.11.cloned.1.call-done = f32[32,512]{1,0:T(8,128)} async-done(((f32[512,512]{1,0:T(8,128)}), f32[32,512]{1,0:T(8,128)}) %reduce-scatter.11.cloned.1.call-update) | async-done | bytes 65552 | tf_op jit(solution)/shard_map/reduce_scatter | solution.py:193
  (959 shorter events, 289.4 us)
Async XLA Ops:
  13.3 185.4 %all-reduce.3.cloned.1.call-start = ((), (), s32[]{:S(2)}) async-start(), calls=%async_computation.8 | async-start | bytes 1048576 | tf_op jit(solution)/shard_map/while/body/eval_jaxpr/psum | solution.py:152
  119.0 83.2 %collective-permute-start.1 = (bf16[256,512]{1,0:T(8,128)(2,1)}, bf16[256,512]{1,0:T(8,128)(2,1)S(1)}, u32[]{:S(2)}, u32[]{:S(2)}) collective-permute-start(bf16[256,512]{1,0:T(8,128)(2,1)} %get-tuple-element.1012), channel_id=1, source_target_pairs={{16,0},{32,16},{48,32},{64,48},{80,64},{96,80},{112,96},{17,1},{33... | collective-permute-start | bytes 786440 | tf_op jit(solution)/shard_map/while/body/eval_jaxpr/ppermute | solution.py:12
  120.3 2.6 copy-start.7
  129.4 71.9 %copy-start.11 = (f32[512,512]{1,0:T(8,128)S(1)}, f32[512,512]{1,0:T(8,128)}, u32[]{:S(2)}) copy-start(f32[512,512]{1,0:T(8,128)} %get-tuple-element.1052) | copy-start | bytes 3145732 | tf_op jit(solution)/shard_map/while
  198.6 2.8 copy-start.25
  200.1 3.4 collective-permute-start
  203.5 184.1 %all-reduce.3.cloned.1.call-start = ((), (), s32[]{:S(2)}) async-start(), calls=%async_computation.8 | async-start | bytes 1048576 | tf_op jit(solution)/shard_map/while/body/eval_jaxpr/psum | solution.py:152
  305.4 85.7 %collective-permute-start.1 = (bf16[256,512]{1,0:T(8,128)(2,1)}, bf16[256,512]{1,0:T(8,128)(2,1)S(1)}, u32[]{:S(2)}, u32[]{:S(2)}) collective-permute-start(bf16[256,512]{1,0:T(8,128)(2,1)} %get-tuple-element.1012), channel_id=1, source_target_pairs={{16,0},{32,16},{48,32},{64,48},{80,64},{96,80},{112,96},{17,1},{33... | collective-permute-start | bytes 786440 | tf_op jit(solution)/shard_map/while/body/eval_jaxpr/ppermute | solution.py:12
  306.7 2.9 copy-start.7
  313.4 1.6 copy-start.21
  317.5 72.8 %copy-start.11 = (f32[512,512]{1,0:T(8,128)S(1)}, f32[512,512]{1,0:T(8,128)}, u32[]{:S(2)}) copy-start(f32[512,512]{1,0:T(8,128)} %get-tuple-element.1052) | copy-start | bytes 3145732 | tf_op jit(solution)/shard_map/while
  387.6 2.8 copy-start.25
  389.0 3.4 collective-permute-start
  392.5 184.1 %all-reduce.3.cloned.1.call-start = ((), (), s32[]{:S(2)}) async-start(), calls=%async_computation.8 | async-start | bytes 1048576 | tf_op jit(solution)/shard_map/while/body/eval_jaxpr/psum | solution.py:152
  494.4 85.7 %collective-permute-start.1 = (bf16[256,512]{1,0:T(8,128)(2,1)}, bf16[256,512]{1,0:T(8,128)(2,1)S(1)}, u32[]{:S(2)}, u32[]{:S(2)}) collective-permute-start(bf16[256,512]{1,0:T(8,128)(2,1)} %get-tuple-element.1012), channel_id=1, source_target_pairs={{16,0},{32,16},{48,32},{64,48},{80,64},{96,80},{112,96},{17,1},{33... | collective-permute-start | bytes 786440 | tf_op jit(solution)/shard_map/while/body/eval_jaxpr/ppermute | solution.py:12
  495.7 2.9 copy-start.7
  506.5 72.8 %copy-start.11 = (f32[512,512]{1,0:T(8,128)S(1)}, f32[512,512]{1,0:T(8,128)}, u32[]{:S(2)}) copy-start(f32[512,512]{1,0:T(8,128)} %get-tuple-element.1052) | copy-start | bytes 3145732 | tf_op jit(solution)/shard_map/while
  576.5 2.8 copy-start.25
  578.0 3.4 collective-permute-start
  581.4 184.1 %all-reduce.3.cloned.1.call-start = ((), (), s32[]{:S(2)}) async-start(), calls=%async_computation.8 | async-start | bytes 1048576 | tf_op jit(solution)/shard_map/while/body/eval_jaxpr/psum | solution.py:152
  683.3 85.7 %collective-permute-start.1 = (bf16[256,512]{1,0:T(8,128)(2,1)}, bf16[256,512]{1,0:T(8,128)(2,1)S(1)}, u32[]{:S(2)}, u32[]{:S(2)}) collective-permute-start(bf16[256,512]{1,0:T(8,128)(2,1)} %get-tuple-element.1012), channel_id=1, source_target_pairs={{16,0},{32,16},{48,32},{64,48},{80,64},{96,80},{112,96},{17,1},{33... | collective-permute-start | bytes 786440 | tf_op jit(solution)/shard_map/while/body/eval_jaxpr/ppermute | solution.py:12
  684.6 2.9 copy-start.7
  695.4 72.8 %copy-start.11 = (f32[512,512]{1,0:T(8,128)S(1)}, f32[512,512]{1,0:T(8,128)}, u32[]{:S(2)}) copy-start(f32[512,512]{1,0:T(8,128)} %get-tuple-element.1052) | copy-start | bytes 3145732 | tf_op jit(solution)/shard_map/while
  765.5 2.8 copy-start.25
  766.9 3.4 collective-permute-start
  770.4 184.1 %all-reduce.3.cloned.1.call-start = ((), (), s32[]{:S(2)}) async-start(), calls=%async_computation.8 | async-start | bytes 1048576 | tf_op jit(solution)/shard_map/while/body/eval_jaxpr/psum | solution.py:152
  872.3 85.7 %collective-permute-start.1 = (bf16[256,512]{1,0:T(8,128)(2,1)}, bf16[256,512]{1,0:T(8,128)(2,1)S(1)}, u32[]{:S(2)}, u32[]{:S(2)}) collective-permute-start(bf16[256,512]{1,0:T(8,128)(2,1)} %get-tuple-element.1012), channel_id=1, source_target_pairs={{16,0},{32,16},{48,32},{64,48},{80,64},{96,80},{112,96},{17,1},{33... | collective-permute-start | bytes 786440 | tf_op jit(solution)/shard_map/while/body/eval_jaxpr/ppermute | solution.py:12
  873.6 2.9 copy-start.7
  880.2 1.6 copy-start.21
  884.4 72.8 %copy-start.11 = (f32[512,512]{1,0:T(8,128)S(1)}, f32[512,512]{1,0:T(8,128)}, u32[]{:S(2)}) copy-start(f32[512,512]{1,0:T(8,128)} %get-tuple-element.1052) | copy-start | bytes 3145732 | tf_op jit(solution)/shard_map/while
  954.4 2.8 copy-start.25
  955.9 3.4 collective-permute-start
  959.3 184.1 %all-reduce.3.cloned.1.call-start = ((), (), s32[]{:S(2)}) async-start(), calls=%async_computation.8 | async-start | bytes 1048576 | tf_op jit(solution)/shard_map/while/body/eval_jaxpr/psum | solution.py:152
  1061.2 85.7 %collective-permute-start.1 = (bf16[256,512]{1,0:T(8,128)(2,1)}, bf16[256,512]{1,0:T(8,128)(2,1)S(1)}, u32[]{:S(2)}, u32[]{:S(2)}) collective-permute-start(bf16[256,512]{1,0:T(8,128)(2,1)} %get-tuple-element.1012), channel_id=1, source_target_pairs={{16,0},{32,16},{48,32},{64,48},{80,64},{96,80},{112,96},{17,1},{33... | collective-permute-start | bytes 786440 | tf_op jit(solution)/shard_map/while/body/eval_jaxpr/ppermute | solution.py:12
  1062.5 2.9 copy-start.7
  1069.2 1.6 copy-start.21
  1073.3 72.8 %copy-start.11 = (f32[512,512]{1,0:T(8,128)S(1)}, f32[512,512]{1,0:T(8,128)}, u32[]{:S(2)}) copy-start(f32[512,512]{1,0:T(8,128)} %get-tuple-element.1052) | copy-start | bytes 3145732 | tf_op jit(solution)/shard_map/while
  1143.4 2.8 copy-start.25
  1144.8 3.4 collective-permute-start
  1148.3 184.1 %all-reduce.3.cloned.1.call-start = ((), (), s32[]{:S(2)}) async-start(), calls=%async_computation.8 | async-start | bytes 1048576 | tf_op jit(solution)/shard_map/while/body/eval_jaxpr/psum | solution.py:152
  1250.2 85.7 %collective-permute-start.1 = (bf16[256,512]{1,0:T(8,128)(2,1)}, bf16[256,512]{1,0:T(8,128)(2,1)S(1)}, u32[]{:S(2)}, u32[]{:S(2)}) collective-permute-start(bf16[256,512]{1,0:T(8,128)(2,1)} %get-tuple-element.1012), channel_id=1, source_target_pairs={{16,0},{32,16},{48,32},{64,48},{80,64},{96,80},{112,96},{17,1},{33... | collective-permute-start | bytes 786440 | tf_op jit(solution)/shard_map/while/body/eval_jaxpr/ppermute | solution.py:12
  1251.5 2.9 copy-start.7
  1258.1 1.6 copy-start.21
  1262.3 72.8 %copy-start.11 = (f32[512,512]{1,0:T(8,128)S(1)}, f32[512,512]{1,0:T(8,128)}, u32[]{:S(2)}) copy-start(f32[512,512]{1,0:T(8,128)} %get-tuple-element.1052) | copy-start | bytes 3145732 | tf_op jit(solution)/shard_map/while
  1332.3 2.8 copy-start.25
  1333.8 3.4 collective-permute-start
  1337.2 184.1 %all-reduce.3.cloned.1.call-start = ((), (), s32[]{:S(2)}) async-start(), calls=%async_computation.8 | async-start | bytes 1048576 | tf_op jit(solution)/shard_map/while/body/eval_jaxpr/psum | solution.py:152
  1439.1 85.7 %collective-permute-start.1 = (bf16[256,512]{1,0:T(8,128)(2,1)}, bf16[256,512]{1,0:T(8,128)(2,1)S(1)}, u32[]{:S(2)}, u32[]{:S(2)}) collective-permute-start(bf16[256,512]{1,0:T(8,128)(2,1)} %get-tuple-element.1012), channel_id=1, source_target_pairs={{16,0},{32,16},{48,32},{64,48},{80,64},{96,80},{112,96},{17,1},{33... | collective-permute-start | bytes 786440 | tf_op jit(solution)/shard_map/while/body/eval_jaxpr/ppermute | solution.py:12
  1440.4 2.9 copy-start.7
  1447.1 1.6 copy-start.21
  1451.2 72.8 %copy-start.11 = (f32[512,512]{1,0:T(8,128)S(1)}, f32[512,512]{1,0:T(8,128)}, u32[]{:S(2)}) copy-start(f32[512,512]{1,0:T(8,128)} %get-tuple-element.1052) | copy-start | bytes 3145732 | tf_op jit(solution)/shard_map/while
  1521.3 2.8 copy-start.25
  1522.7 3.4 collective-permute-start
  1526.2 184.1 %all-reduce.3.cloned.1.call-start = ((), (), s32[]{:S(2)}) async-start(), calls=%async_computation.8 | async-start | bytes 1048576 | tf_op jit(solution)/shard_map/while/body/eval_jaxpr/psum | solution.py:152
  1628.1 85.7 %collective-permute-start.1 = (bf16[256,512]{1,0:T(8,128)(2,1)}, bf16[256,512]{1,0:T(8,128)(2,1)S(1)}, u32[]{:S(2)}, u32[]{:S(2)}) collective-permute-start(bf16[256,512]{1,0:T(8,128)(2,1)} %get-tuple-element.1012), channel_id=1, source_target_pairs={{16,0},{32,16},{48,32},{64,48},{80,64},{96,80},{112,96},{17,1},{33... | collective-permute-start | bytes 786440 | tf_op jit(solution)/shard_map/while/body/eval_jaxpr/ppermute | solution.py:12
  1629.4 2.9 copy-start.7
  1636.0 1.6 copy-start.21
  1640.2 72.8 %copy-start.11 = (f32[512,512]{1,0:T(8,128)S(1)}, f32[512,512]{1,0:T(8,128)}, u32[]{:S(2)}) copy-start(f32[512,512]{1,0:T(8,128)} %get-tuple-element.1052) | copy-start | bytes 3145732 | tf_op jit(solution)/shard_map/while
  1710.2 2.8 copy-start.25
  1711.7 3.4 collective-permute-start
  1715.1 80.0 %reduce-scatter.5.cloned.1.call-start = ((), (), s32[]{:S(2)}) async-start(), calls=%async_computation.4 | async-start | bytes 1114112 | tf_op jit(solution)/shard_map/reduce_scatter | solution.py:190
  1715.7 155.7 %reduce-scatter.7.cloned.1.call-start = ((), (), s32[]{:S(2)}) async-start(), calls=%async_computation.5 | async-start | bytes 1114112 | tf_op jit(solution)/shard_map/reduce_scatter | solution.py:191
  1716.3 231.1 %reduce-scatter.9.cloned.1.call-start = ((), (), s32[]{:S(2)}) async-start(), calls=%async_computation.6 | async-start | bytes 1114112 | tf_op jit(solution)/shard_map/reduce_scatter | solution.py:192
  1716.9 307.1 %reduce-scatter.11.cloned.1.call-start = ((), (), s32[]{:S(2)}) async-start(), calls=%async_computation.7 | async-start | bytes 1114112 | tf_op jit(solution)/shard_map/reduce_scatter | solution.py:193
  (251 other events, 283.4 us)
Sparse Core Ops, SparseCore 0:
  115.9 82.6 all-reduce.2
  302.4 85.1 all-reduce.2
  491.3 85.1 all-reduce.2
  680.3 85.1 all-reduce.2
  869.2 85.1 all-reduce.2
  1058.2 85.1 all-reduce.2
  1247.1 85.1 all-reduce.2
  1436.1 85.1 all-reduce.2
  1625.0 85.1 all-reduce.2
Sparse Core Ops, SparseCore 1:
  1719.4 75.7 reduce-scatter.4
  1799.1 72.2 reduce-scatter.6
  1875.0 72.3 reduce-scatter.8
  1951.5 72.4 reduce-scatter.10
where the time goes:
time: 2040 us; the launch traced here: 2030 us
  waiting for transfers between devices  946 us (46%)
  blocking collectives  702 us (34%)
  matrix products  214 us (10%)
  local copies, waits for them, and re-layouts  123 us (6%)
  starting transfers between devices  23.3 us (1%)
    psum x9, blocking collectives, advance(): aggregate = lax.psum(partial_agg, 'edge')  702 us
    psum x9, waiting for transfers between devices, advance(): edge_terms = lax.psum(partial_back, 'edge')  630 us
    while x558, local copies, waits for them, and re-layouts  96.3 us
    reduce_scatter x1, waiting for transfers between devices, body(): lax.psum_scatter(sum_msg, 'edge', scatter_dimension=0, tiled=True)  76.5 us
    reduce_scatter x1, waiting for transfers between devices, body(): lax.psum_scatter(sum_recv, 'edge', scatter_dimension=0, tiled=True)  76.3 us
    reduce_scatter x1, waiting for transfers between devices, body(): lax.psum_scatter(sum_edge, 'edge', scatter_dimension=0, tiled=True)  76 us
    reduce_scatter x1, waiting for transfers between devices, body(): lax.psum_scatter(sum_send, 'edge', scatter_dimension=0, tiled=True)  73.1 us
    dot_general x63, matrix products, transposed_times(): lax.dot_general(left, right, (((0,), (0,)), ((), ())), preferred_element_...  70.9 us
  transfers between devices with their start and end apart: 31, of which 22 were waited for; matrix products, arithmetic and copies ran while one was open for 5% of the time, Pallas kernels for 0%

commit v1 on v0

--- a/solution.py
+++ b/solution.py
@@ -125,7 +125,11 @@
         act = jax.nn.silu(pre).astype(jnp.bfloat16)
         message = matmul(act, weight_msg).astype(jnp.bfloat16)
         partial_agg = to_nodes(message, recv_blocks, recv_tiles)
-        aggregate = lax.psum(partial_agg, "edge")
+        aggregate = partial_agg
+        for hop in (1, 2, 4, 8):
+            aggregate = aggregate + lax.ppermute(
+                aggregate, "edge", [(dev, dev ^ hop) for dev in range(16)]
+            )
         agg_b = aggregate.astype(jnp.bfloat16)
         node_pre = matmul(feats, weight_node) + matmul(agg_b, weight_agg)
         node_act = jax.nn.silu(node_pre).astype(jnp.bfloat16)

time: 2040 us -> 1860 us (0.912)
  blocking collectives: 702 us -> 0 us
  waiting for transfers between devices: 946 us -> 1420 us
  starting transfers between devices: 23.3 us -> 82.8 us
  other arithmetic: 2.35 us -> 24 us
  local copies, waits for them, and re-layouts: 123 us -> 102 us
    psum x9 -> x0, blocking collectives: 702 us -> none  [advance(): aggregate = lax.psum(partial_agg, 'edge')]
    ppermute x0 -> x36, waiting for transfers between devices: none -> 430 us  [advance(): lax.ppermute(aggregate, 'edge', [(dev, dev ^ hop) for dev in range(16)])]
    ppermute x0 -> x36, starting transfers between devices: none -> 59.5 us  [advance(): lax.ppermute(aggregate, 'edge', [(dev, dev ^ hop) for dev in range(16)])]
    psum x9, waiting for transfers between devices: 630 us -> 669 us  [advance(): edge_terms = lax.psum(partial_back, 'edge')]
    while x558 -> x576, local copies, waits for them, and re-layouts: 96.3 us -> 74.5 us
  transfers between devices with their start and end apart: 31 -> 67, of which waited for: 22 -> 58; matrix products, arithmetic and copies ran while one was open for 5% -> 6% of each run, Pallas kernels for 0% -> 0%
where the time goes in v1:
time: 1860 us
  waiting for transfers between devices  1420 us (76%)
  matrix products  214 us (12%)
  local copies, waits for them, and re-layouts  102 us (5%)
  starting transfers between devices  82.8 us (4%)
  other arithmetic  24 us (1%)
    psum x9, waiting for transfers between devices, advance(): edge_terms = lax.psum(partial_back, 'edge')  669 us
    ppermute x36, waiting for transfers between devices, advance(): lax.ppermute(aggregate, 'edge', [(dev, dev ^ hop) for dev in range(16)])  430 us
    reduce_scatter x1, waiting for transfers between devices, body(): lax.psum_scatter(sum_msg, 'edge', scatter_dimension=0, tiled=True)  76.5 us
    reduce_scatter x1, waiting for transfers between devices, body(): lax.psum_scatter(sum_recv, 'edge', scatter_dimension=0, tiled=True)  76.3 us
    reduce_scatter x1, waiting for transfers between devices, body(): lax.psum_scatter(sum_edge, 'edge', scatter_dimension=0, tiled=True)  76 us
    while x576, local copies, waits for them, and re-layouts  74.5 us
    reduce_scatter x1, waiting for transfers between devices, body(): lax.psum_scatter(sum_send, 'edge', scatter_dimension=0, tiled=True)  73.2 us
    dot_general x63, matrix products, transposed_times(): lax.dot_general(left, right, (((0,), (0,)), ((), ())), preferred_element_...  71.2 us
  transfers between devices with their start and end apart: 67, of which 58 were waited for; matrix products, arithmetic and copies ran while one was open for 6% of the time, Pallas kernels for 0%

profile of v1, /device:TPU:0, one launch (start us, length us, event | category | flops | bytes accessed | tf_op | source)
XLA Modules:
  0.0 1858.3 jit_solution(995033740483376372)
XLA Ops:
  14.2 1528.0 %while.36 = (s32[]{:T(128)}, bf16[256,512]{1,0:T(8,128)(2,1)}, bf16[256,512]{1,0:T(8,128)(2,1)}, f32[512,512]{1,0:T(8,128)}, f32[512,512]{1,0:T(8,128)}, /*index...) while((s32[]{:T(128)}, bf16[256,512]{1,0:T(8,128)(2,1)}, ...), condition=%wide.region_2.3_spmd.clone, body=%wide.region_0.2_spmd.clone.sunk | while | flops 2910724096 | bytes 153275056 | solution.py:190
  23.7 11.9 collective-permute-done
  35.8 3.4 collective-permute-start.1
  39.1 11.0 collective-permute-done.1
  52.5 10.1 collective-permute-done.2
  62.7 4.3 collective-permute-start.3
  68.4 8.8 collective-permute-done.3
  101.7 73.3 %all-reduce.2.cloned.1.call-done = f32[256,512]{1,0:T(8,128)} async-done(((f32[256,512]{1,0:T(8,128)}), f32[256,512]{1,0:T(8,128)}) %all-reduce.2.cloned.1.call-update) | async-done | bytes 524304 | tf_op jit(solution)/shard_map/while/body/eval_jaxpr/psum | solution.py:156
  189.6 10.5 collective-permute-done
  202.1 12.2 collective-permute-done.1
  215.6 12.6 collective-permute-done.2
  231.4 13.3 collective-permute-done.3
  256.6 2.9 add_select_fusion.17
  268.2 2.6 add_select_fusion.20
  270.8 74.4 %all-reduce.2.cloned.1.call-done = f32[256,512]{1,0:T(8,128)} async-done(((f32[256,512]{1,0:T(8,128)}), f32[256,512]{1,0:T(8,128)}) %all-reduce.2.cloned.1.call-update) | async-done | bytes 524304 | tf_op jit(solution)/shard_map/while/body/eval_jaxpr/psum | solution.py:156
  359.7 10.5 collective-permute-done
  372.3 12.2 collective-permute-done.1
  385.8 12.6 collective-permute-done.2
  401.5 13.2 collective-permute-done.3
  426.8 2.9 add_select_fusion.17
  438.3 2.6 add_select_fusion.20
  440.9 74.5 %all-reduce.2.cloned.1.call-done = f32[256,512]{1,0:T(8,128)} async-done(((f32[256,512]{1,0:T(8,128)}), f32[256,512]{1,0:T(8,128)}) %all-reduce.2.cloned.1.call-update) | async-done | bytes 524304 | tf_op jit(solution)/shard_map/while/body/eval_jaxpr/psum | solution.py:156
  530.0 10.5 collective-permute-done
  542.5 12.2 collective-permute-done.1
  556.0 12.6 collective-permute-done.2
  571.7 13.2 collective-permute-done.3
  597.0 2.9 add_select_fusion.17
  611.1 74.5 %all-reduce.2.cloned.1.call-done = f32[256,512]{1,0:T(8,128)} async-done(((f32[256,512]{1,0:T(8,128)}), f32[256,512]{1,0:T(8,128)}) %all-reduce.2.cloned.1.call-update) | async-done | bytes 524304 | tf_op jit(solution)/shard_map/while/body/eval_jaxpr/psum | solution.py:156
  700.2 10.5 collective-permute-done
  712.7 12.2 collective-permute-done.1
  726.2 12.6 collective-permute-done.2
  742.0 13.2 collective-permute-done.3
  767.2 2.9 add_select_fusion.17
  778.7 2.6 add_select_fusion.20
  781.3 74.5 %all-reduce.2.cloned.1.call-done = f32[256,512]{1,0:T(8,128)} async-done(((f32[256,512]{1,0:T(8,128)}), f32[256,512]{1,0:T(8,128)}) %all-reduce.2.cloned.1.call-update) | async-done | bytes 524304 | tf_op jit(solution)/shard_map/while/body/eval_jaxpr/psum | solution.py:156
  870.4 10.5 collective-permute-done
  882.9 12.2 collective-permute-done.1
  896.4 12.6 collective-permute-done.2
  912.2 13.2 collective-permute-done.3
  937.4 2.9 add_select_fusion.17
  948.9 2.6 add_select_fusion.20
  951.5 74.5 %all-reduce.2.cloned.1.call-done = f32[256,512]{1,0:T(8,128)} async-done(((f32[256,512]{1,0:T(8,128)}), f32[256,512]{1,0:T(8,128)}) %all-reduce.2.cloned.1.call-update) | async-done | bytes 524304 | tf_op jit(solution)/shard_map/while/body/eval_jaxpr/psum | solution.py:156
  1040.6 10.5 collective-permute-done
  1053.1 12.2 collective-permute-done.1
  1066.6 12.6 collective-permute-done.2
  1082.4 13.2 collective-permute-done.3
  1107.6 2.9 add_select_fusion.17
  1121.7 74.5 %all-reduce.2.cloned.1.call-done = f32[256,512]{1,0:T(8,128)} async-done(((f32[256,512]{1,0:T(8,128)}), f32[256,512]{1,0:T(8,128)}) %all-reduce.2.cloned.1.call-update) | async-done | bytes 524304 | tf_op jit(solution)/shard_map/while/body/eval_jaxpr/psum | solution.py:156
  1210.8 10.5 collective-permute-done
  1223.3 12.2 collective-permute-done.1
  1236.8 12.6 collective-permute-done.2
  1252.6 13.2 collective-permute-done.3
  1277.8 2.9 add_select_fusion.17
  1291.9 74.5 %all-reduce.2.cloned.1.call-done = f32[256,512]{1,0:T(8,128)} async-done(((f32[256,512]{1,0:T(8,128)}), f32[256,512]{1,0:T(8,128)}) %all-reduce.2.cloned.1.call-update) | async-done | bytes 524304 | tf_op jit(solution)/shard_map/while/body/eval_jaxpr/psum | solution.py:156
  1381.0 10.5 collective-permute-done
  1393.5 12.2 collective-permute-done.1
  1407.0 12.6 collective-permute-done.2
  1422.8 13.2 collective-permute-done.3
  1448.0 2.9 add_select_fusion.17
  1462.1 74.5 %all-reduce.2.cloned.1.call-done = f32[256,512]{1,0:T(8,128)} async-done(((f32[256,512]{1,0:T(8,128)}), f32[256,512]{1,0:T(8,128)}) %all-reduce.2.cloned.1.call-update) | async-done | bytes 524304 | tf_op jit(solution)/shard_map/while/body/eval_jaxpr/psum | solution.py:156
  1549.1 73.2 %reduce-scatter.5.cloned.1.call-done = f32[32,512]{1,0:T(8,128)} async-done(((f32[512,512]{1,0:T(8,128)}), f32[32,512]{1,0:T(8,128)}) %reduce-scatter.5.cloned.1.call-update) | async-done | bytes 65552 | tf_op jit(solution)/shard_map/reduce_scatter | solution.py:194
  1622.2 76.3 %reduce-scatter.7.cloned.1.call-done = f32[32,512]{1,0:T(8,128)} async-done(((f32[512,512]{1,0:T(8,128)}), f32[32,512]{1,0:T(8,128)}) %reduce-scatter.7.cloned.1.call-update) | async-done | bytes 65552 | tf_op jit(solution)/shard_map/reduce_scatter | solution.py:195
  1698.5 76.0 %reduce-scatter.9.cloned.1.call-done = f32[32,512]{1,0:T(8,128)} async-done(((f32[512,512]{1,0:T(8,128)}), f32[32,512]{1,0:T(8,128)}) %reduce-scatter.9.cloned.1.call-update) | async-done | bytes 65552 | tf_op jit(solution)/shard_map/reduce_scatter | solution.py:196
  1774.5 76.5 %reduce-scatter.11.cloned.1.call-done = f32[32,512]{1,0:T(8,128)} async-done(((f32[512,512]{1,0:T(8,128)}), f32[32,512]{1,0:T(8,128)}) %reduce-scatter.11.cloned.1.call-update) | async-done | bytes 65552 | tf_op jit(solution)/shard_map/reduce_scatter | solution.py:197
  (1076 shorter events, 395.9 us)
Async XLA Ops:
  14.2 160.8 %all-reduce.2.cloned.1.call-start = ((), (), s32[]{:S(2)}) async-start(), calls=%async_computation.8 | async-start | bytes 1048576 | tf_op jit(solution)/shard_map/while/body/eval_jaxpr/psum | solution.py:156
  22.1 13.6 collective-permute-start
  35.8 14.4 collective-permute-start.1
  50.2 12.4 collective-permute-start.2
  62.7 14.4 collective-permute-start.3
  97.5 81.1 %collective-permute-start.5 = (bf16[256,512]{1,0:T(8,128)(2,1)}, bf16[256,512]{1,0:T(8,128)(2,1)}, u32[]{:S(2)}, u32[]{:S(2)}) collective-permute-start(bf16[256,512]{1,0:T(8,128)(2,1)} %get-tuple-element.1012), channel_id=1, source_target_pairs={{16,0},{32,16},{48,32},{64,48},{80,64},{96,80},{112,96},{17,1},{33... | collective-permute-start | bytes 786440 | tf_op jit(solution)/shard_map/while/body/eval_jaxpr/ppermute | solution.py:12
  176.4 3.4 collective-permute-start.4
  180.6 164.6 %all-reduce.2.cloned.1.call-start = ((), (), s32[]{:S(2)}) async-start(), calls=%async_computation.8 | async-start | bytes 1048576 | tf_op jit(solution)/shard_map/while/body/eval_jaxpr/psum | solution.py:156
  188.4 11.6 collective-permute-start
  200.1 14.2 collective-permute-start.1
  214.4 13.8 collective-permute-start.2
  228.3 16.3 collective-permute-start.3
  265.3 83.4 %collective-permute-start.5 = (bf16[256,512]{1,0:T(8,128)(2,1)}, bf16[256,512]{1,0:T(8,128)(2,1)}, u32[]{:S(2)}, u32[]{:S(2)}) collective-permute-start(bf16[256,512]{1,0:T(8,128)(2,1)} %get-tuple-element.1012), channel_id=1, source_target_pairs={{16,0},{32,16},{48,32},{64,48},{80,64},{96,80},{112,96},{17,1},{33... | collective-permute-start | bytes 786440 | tf_op jit(solution)/shard_map/while/body/eval_jaxpr/ppermute | solution.py:12
  346.6 3.4 collective-permute-start.4
  350.7 164.6 %all-reduce.2.cloned.1.call-start = ((), (), s32[]{:S(2)}) async-start(), calls=%async_computation.8 | async-start | bytes 1048576 | tf_op jit(solution)/shard_map/while/body/eval_jaxpr/psum | solution.py:156
  358.6 11.6 collective-permute-start
  370.3 14.2 collective-permute-start.1
  384.6 13.8 collective-permute-start.2
  398.5 16.3 collective-permute-start.3
  435.5 83.5 %collective-permute-start.5 = (bf16[256,512]{1,0:T(8,128)(2,1)}, bf16[256,512]{1,0:T(8,128)(2,1)}, u32[]{:S(2)}, u32[]{:S(2)}) collective-permute-start(bf16[256,512]{1,0:T(8,128)(2,1)} %get-tuple-element.1012), channel_id=1, source_target_pairs={{16,0},{32,16},{48,32},{64,48},{80,64},{96,80},{112,96},{17,1},{33... | collective-permute-start | bytes 786440 | tf_op jit(solution)/shard_map/while/body/eval_jaxpr/ppermute | solution.py:12
  520.9 164.6 %all-reduce.2.cloned.1.call-start = ((), (), s32[]{:S(2)}) async-start(), calls=%async_computation.8 | async-start | bytes 1048576 | tf_op jit(solution)/shard_map/while/body/eval_jaxpr/psum | solution.py:156
  528.8 11.6 collective-permute-start
  540.5 14.2 collective-permute-start.1
  554.8 13.8 collective-permute-start.2
  568.7 16.3 collective-permute-start.3
  605.7 83.5 %collective-permute-start.5 = (bf16[256,512]{1,0:T(8,128)(2,1)}, bf16[256,512]{1,0:T(8,128)(2,1)}, u32[]{:S(2)}, u32[]{:S(2)}) collective-permute-start(bf16[256,512]{1,0:T(8,128)(2,1)} %get-tuple-element.1012), channel_id=1, source_target_pairs={{16,0},{32,16},{48,32},{64,48},{80,64},{96,80},{112,96},{17,1},{33... | collective-permute-start | bytes 786440 | tf_op jit(solution)/shard_map/while/body/eval_jaxpr/ppermute | solution.py:12
  687.0 3.4 collective-permute-start.4
  691.2 164.6 %all-reduce.2.cloned.1.call-start = ((), (), s32[]{:S(2)}) async-start(), calls=%async_computation.8 | async-start | bytes 1048576 | tf_op jit(solution)/shard_map/while/body/eval_jaxpr/psum | solution.py:156
  699.0 11.6 collective-permute-start
  710.7 14.2 collective-permute-start.1
  725.0 13.8 collective-permute-start.2
  738.9 16.3 collective-permute-start.3
  775.9 83.5 %collective-permute-start.5 = (bf16[256,512]{1,0:T(8,128)(2,1)}, bf16[256,512]{1,0:T(8,128)(2,1)}, u32[]{:S(2)}, u32[]{:S(2)}) collective-permute-start(bf16[256,512]{1,0:T(8,128)(2,1)} %get-tuple-element.1012), channel_id=1, source_target_pairs={{16,0},{32,16},{48,32},{64,48},{80,64},{96,80},{112,96},{17,1},{33... | collective-permute-start | bytes 786440 | tf_op jit(solution)/shard_map/while/body/eval_jaxpr/ppermute | solution.py:12
  857.2 3.4 collective-permute-start.4
  861.4 164.6 %all-reduce.2.cloned.1.call-start = ((), (), s32[]{:S(2)}) async-start(), calls=%async_computation.8 | async-start | bytes 1048576 | tf_op jit(solution)/shard_map/while/body/eval_jaxpr/psum | solution.py:156
  869.2 11.6 collective-permute-start
  880.9 14.2 collective-permute-start.1
  895.2 13.8 collective-permute-start.2
  909.1 16.3 collective-permute-start.3
  946.1 83.5 %collective-permute-start.5 = (bf16[256,512]{1,0:T(8,128)(2,1)}, bf16[256,512]{1,0:T(8,128)(2,1)}, u32[]{:S(2)}, u32[]{:S(2)}) collective-permute-start(bf16[256,512]{1,0:T(8,128)(2,1)} %get-tuple-element.1012), channel_id=1, source_target_pairs={{16,0},{32,16},{48,32},{64,48},{80,64},{96,80},{112,96},{17,1},{33... | collective-permute-start | bytes 786440 | tf_op jit(solution)/shard_map/while/body/eval_jaxpr/ppermute | solution.py:12
  1027.4 3.4 collective-permute-start.4
  1031.6 164.6 %all-reduce.2.cloned.1.call-start = ((), (), s32[]{:S(2)}) async-start(), calls=%async_computation.8 | async-start | bytes 1048576 | tf_op jit(solution)/shard_map/while/body/eval_jaxpr/psum | solution.py:156
  1039.4 11.6 collective-permute-start
  1051.1 14.2 collective-permute-start.1
  1065.4 13.8 collective-permute-start.2
  1079.3 16.3 collective-permute-start.3
  1116.3 83.5 %collective-permute-start.5 = (bf16[256,512]{1,0:T(8,128)(2,1)}, bf16[256,512]{1,0:T(8,128)(2,1)}, u32[]{:S(2)}, u32[]{:S(2)}) collective-permute-start(bf16[256,512]{1,0:T(8,128)(2,1)} %get-tuple-element.1012), channel_id=1, source_target_pairs={{16,0},{32,16},{48,32},{64,48},{80,64},{96,80},{112,96},{17,1},{33... | collective-permute-start | bytes 786440 | tf_op jit(solution)/shard_map/while/body/eval_jaxpr/ppermute | solution.py:12
  1197.6 3.4 collective-permute-start.4
  1201.8 164.6 %all-reduce.2.cloned.1.call-start = ((), (), s32[]{:S(2)}) async-start(), calls=%async_computation.8 | async-start | bytes 1048576 | tf_op jit(solution)/shard_map/while/body/eval_jaxpr/psum | solution.py:156
  1209.6 11.6 collective-permute-start
  1221.3 14.2 collective-permute-start.1
  1235.6 13.8 collective-permute-start.2
  1249.5 16.3 collective-permute-start.3
  1286.5 83.5 %collective-permute-start.5 = (bf16[256,512]{1,0:T(8,128)(2,1)}, bf16[256,512]{1,0:T(8,128)(2,1)}, u32[]{:S(2)}, u32[]{:S(2)}) collective-permute-start(bf16[256,512]{1,0:T(8,128)(2,1)} %get-tuple-element.1012), channel_id=1, source_target_pairs={{16,0},{32,16},{48,32},{64,48},{80,64},{96,80},{112,96},{17,1},{33... | collective-permute-start | bytes 786440 | tf_op jit(solution)/shard_map/while/body/eval_jaxpr/ppermute | solution.py:12
  1372.0 164.6 %all-reduce.2.cloned.1.call-start = ((), (), s32[]{:S(2)}) async-start(), calls=%async_computation.8 | async-start | bytes 1048576 | tf_op jit(solution)/shard_map/while/body/eval_jaxpr/psum | solution.py:156
  1379.8 11.6 collective-permute-start
  1391.5 14.2 collective-permute-start.1
  1405.8 13.8 collective-permute-start.2
  1419.7 16.3 collective-permute-start.3
  1456.7 83.5 %collective-permute-start.5 = (bf16[256,512]{1,0:T(8,128)(2,1)}, bf16[256,512]{1,0:T(8,128)(2,1)}, u32[]{:S(2)}, u32[]{:S(2)}) collective-permute-start(bf16[256,512]{1,0:T(8,128)(2,1)} %get-tuple-element.1012), channel_id=1, source_target_pairs={{16,0},{32,16},{48,32},{64,48},{80,64},{96,80},{112,96},{17,1},{33... | collective-permute-start | bytes 786440 | tf_op jit(solution)/shard_map/while/body/eval_jaxpr/ppermute | solution.py:12
  1542.2 80.1 %reduce-scatter.5.cloned.1.call-start = ((), (), s32[]{:S(2)}) async-start(), calls=%async_computation.4 | async-start | bytes 1114112 | tf_op jit(solution)/shard_map/reduce_scatter | solution.py:194
  1542.7 155.8 %reduce-scatter.7.cloned.1.call-start = ((), (), s32[]{:S(2)}) async-start(), calls=%async_computation.5 | async-start | bytes 1114112 | tf_op jit(solution)/shard_map/reduce_scatter | solution.py:195
  1543.3 231.2 %reduce-scatter.9.cloned.1.call-start = ((), (), s32[]{:S(2)}) async-start(), calls=%async_computation.6 | async-start | bytes 1114112 | tf_op jit(solution)/shard_map/reduce_scatter | solution.py:196
  1543.9 307.1 %reduce-scatter.11.cloned.1.call-start = ((), (), s32[]{:S(2)}) async-start(), calls=%async_computation.7 | async-start | bytes 1114112 | tf_op jit(solution)/shard_map/reduce_scatter | solution.py:197
  (296 other events, 2182.4 us)
Sparse Core Ops, SparseCore 0:
  89.3 85.6 all-reduce.1
  256.8 88.3 all-reduce.1
  426.9 88.4 all-reduce.1
  597.1 88.4 all-reduce.1
  767.3 88.4 all-reduce.1
  937.5 88.4 all-reduce.1
  1107.7 88.4 all-reduce.1
  1277.9 88.4 all-reduce.1
  1448.1 88.4 all-reduce.1
Sparse Core Ops, SparseCore 1:
  1546.4 75.8 reduce-scatter.4
  1626.2 72.3 reduce-scatter.6
  1702.2 72.3 reduce-scatter.8
  1778.6 72.3 reduce-scatter.10
